TPU v7x, 512 devices: a whole 4x8x8 slice. The times are simulated.
512 devices in a mesh: fsdp: 32 (over z, y_lo, core), dp: 4 (over y_hi), tensor: 4 (over x).
Axes of the slice: x: 4, y: 8 (y_hi: 4, y_lo: 2; y = y_hi * 2 + y_lo), z: 8, core: 2. Of those that a mesh axis runs over, the one named last changes fastest.
Arguments:
- master_weight: float32 [4096, 14336], P(('fsdp', 'dp'), 'tensor'), may hold values from -0.09375 to 0.09375
- first_moment: bfloat16 [4096, 14336], P(('fsdp', 'dp'), 'tensor'), may hold values from -6 to 6
- second_moment: bfloat16 [4096, 14336], P(('fsdp', 'dp'), 'tensor'), may hold values from 0.25 to 16
- teacher_weight: float32 [4096, 14336], P(('fsdp', 'dp'), 'tensor'), may hold values from -0.09375 to 0.09375
- grad_parts: bfloat16 [4, 4096, 14336], P('dp', 'fsdp', 'tensor'), may hold values from -6 to 6
- embed_table: bfloat16 [4096, 64128], P(('fsdp', 'dp', 'tensor')), may hold values from -6 to 6
- token_ids: int32 [32, 256], P('fsdp'), may hold values from 0 to 64127
- pair_ids: int32 [32, 256], P('fsdp'), may hold values from 0 to 7, never falling along the last dimension, each value on 1 to 64 neighbouring positions
- class_head: bfloat16 [4, 3584, 256], P('tensor', 'dp'), may hold values from -0.046875 to 0.046875
Outputs:
- master_new: float32 [4096, 14336], P(('fsdp', 'dp'), 'tensor')
- first_new: bfloat16 [4096, 14336], P(('fsdp', 'dp'), 'tensor')
- second_new: bfloat16 [4096, 14336], P(('fsdp', 'dp'), 'tensor')
- teacher_new: float32 [4096, 14336], P(('fsdp', 'dp'), 'tensor')
- class_logits: float32 [32, 8, 256], P('fsdp')
Inputs may be any that keep to these rules, and one draw needn't show every extreme that they name: `pair_ids`: in every row the pair numbers never fall, and each of the 8 pairs holds 1 to 64 tokens, one of them exactly 64.
All inputs are finite; a program needn't handle non-finite values.
Results may differ from a plain program's by a relative error of at most 0.0055.
Values may be sent and summed in bfloat16 or wider, within the bound.
No kernel may reach another device: no remote copies, remote signals or barrier semaphores. Data moves between devices by JAX's collectives and lax.ppermute only.
A program may use at most 128 MiB of HBM per device.

v0:
```python
import jax
import jax.numpy as jnp
from jax import lax
from jax.sharding import PartitionSpec as P

PAIRS = 8
beta_one = 0.9
beta_two = 0.95
learn_rate = 0.001
decay_rate = 0.1
ema_keep = 0.99


def optimizer_step(master_weight, first_moment, second_moment, teacher_weight, grad_parts):
    gradient = lax.psum_scatter(grad_parts[0], "dp", scatter_dimension=0, tiled=True).astype(
        jnp.float32
    )
    first_full = beta_one * first_moment.astype(jnp.float32) + (1.0 - beta_one) * gradient
    second_full = (
        beta_two * second_moment.astype(jnp.float32) + (1.0 - beta_two) * gradient * gradient
    )
    master_new = master_weight - learn_rate * (
        first_full / (jnp.sqrt(second_full) + 1e-08) + decay_rate * master_weight
    )
    teacher_new = ema_keep * teacher_weight + (1.0 - ema_keep) * master_new
    return (
        master_new,
        first_full.astype(jnp.bfloat16),
        second_full.astype(jnp.bfloat16),
        teacher_new,
    )


def ring_gather(block, axis):
    count = lax.axis_size(axis)
    right = [(i, (i + 1) % count) for i in range(count)]
    left = [(i, (i - 1) % count) for i in range(count)]
    place = lax.axis_index(axis)
    half = block.shape[0] // 2
    whole = jnp.zeros((count,) + block.shape, block.dtype)
    whole = lax.dynamic_update_index_in_dim(whole, block, place, 0)
    going_right = going_left = block
    for step in range(1, count // 2):
        going_right = lax.ppermute(going_right, axis, right)
        going_left = lax.ppermute(going_left, axis, left)
        whole = lax.dynamic_update_index_in_dim(whole, going_right, (place - step) % count, 0)
        whole = lax.dynamic_update_index_in_dim(whole, going_left, (place + step) % count, 0)
    first = lax.ppermute(going_right[:half], axis, right)
    second = lax.ppermute(going_left[half:], axis, left)
    last = jnp.concatenate([first, second], axis=0)
    return lax.dynamic_update_index_in_dim(whole, last, (place + count // 2) % count, 0)


def embed_inputs(embed_table, token_ids):
    every_id = lax.all_to_all(
        jnp.broadcast_to(token_ids, (32, token_ids.shape[1])), "fsdp", 0, 0, tiled=True
    )
    picked = embed_table.at[:, every_id.reshape(-1)].get(mode="promise_in_bounds")
    received = lax.all_to_all(
        picked.reshape(8, 32, 256).transpose(1, 0, 2),
        "fsdp",
        split_axis=0,
        concat_axis=0,
        tiled=True,
    )
    part = lax.all_gather(received.reshape(256, 256), "dp", axis=0, tiled=True)
    return ring_gather(part, "tensor")


def label_tokens(teacher_new, stacked, group_pairs, class_head):
    teacher_half = teacher_new.astype(jnp.bfloat16)
    replica_count = lax.axis_size("dp")
    rows = teacher_half.shape[0]
    width = teacher_half.shape[1] // replica_count
    split = teacher_half.reshape(rows, replica_count, width).transpose(1, 0, 2)
    block = lax.all_to_all(split.reshape(-1, width), "dp", 0, 0, tiled=True)
    row_block = lax.all_gather(block, "fsdp", axis=0, tiled=True)
    inputs = stacked.reshape(4, 4, 32, 8, 256).transpose(2, 1, 0, 3, 4).reshape(4096, 256)
    values = inputs.astype(jnp.float32)
    scale = lax.rsqrt(jnp.mean(values * values, axis=0, keepdims=True) + 1e-05)
    normed = (values * scale).astype(jnp.bfloat16)
    hidden = jnp.einsum("fk,fo->ko", normed, row_block, preferred_element_type=jnp.float32)
    group_count = group_pairs.shape[0]
    active = jax.nn.silu(hidden).reshape(group_count, -1, width)
    member_of = (
        group_pairs[:, None, :] == jnp.arange(PAIRS, dtype=jnp.int32)[None, :, None]
    ).astype(jnp.float32)
    totals = jnp.einsum("gpt,gtk->gpk", member_of, active, precision=lax.Precision.HIGHEST)
    pooled = (totals / jnp.sum(member_of, axis=2, keepdims=True)).astype(jnp.bfloat16)
    head_part = class_head[0]
    partial_terms = jnp.einsum("gpk,kc->gpc", pooled, head_part, preferred_element_type=jnp.float32)
    return lax.psum(lax.psum(partial_terms, "dp"), "tensor")


def shards(
    master_weight,
    first_moment,
    second_moment,
    teacher_weight,
    grad_parts,
    embed_table,
    token_ids,
    pair_ids,
    class_head,
):
    master_new, first_new, second_new, teacher_new = optimizer_step(
        master_weight, first_moment, second_moment, teacher_weight, grad_parts
    )
    stacked = embed_inputs(embed_table, token_ids)
    class_logits = label_tokens(teacher_new, stacked, pair_ids, class_head)
    return (master_new, first_new, second_new, teacher_new, class_logits)


def solution(mesh):
    placed = (
        P(("fsdp", "dp"), "tensor"),
        P(("fsdp", "dp"), "tensor"),
        P(("fsdp", "dp"), "tensor"),
        P(("fsdp", "dp"), "tensor"),
        P("dp", "fsdp", "tensor"),
        P(("fsdp", "dp", "tensor"), None),
        P("fsdp", None),
        P("fsdp", None),
        P("tensor", "dp", None),
    )
    return jax.shard_map(
        shards,
        mesh=mesh,
        in_specs=placed,
        out_specs=(
            P(("fsdp", "dp"), "tensor"),
            P(("fsdp", "dp"), "tensor"),
            P(("fsdp", "dp"), "tensor"),
            P(("fsdp", "dp"), "tensor"),
            P("fsdp", None, None),
        ),
        check_vma=False,
    )
```

profile of v0, /device:TPU:8, one launch (start us, length us, event | category | flops | bytes accessed | tf_op | source)
XLA Modules:
  0.0 217.0 jit_solution(6691346589471912774)
XLA Ops:
  7.2 0.0 copy-start
  7.2 0.0 reduce-scatter.2.cloned.1.call-start
  7.2 0.7 reduce-scatter.2.cloned.1.call-update
  7.9 0.0 copy-start.2
  7.9 0.0 copy-start.1
  7.9 0.0 all-gather.2.cloned.1.call-start
  8.0 42.5 %reduce-scatter.2.cloned.1.call-done = bf16[32,3584]{1,0:T(8,128)(2,1)} async-done(((bf16[128,3584]{1,0:T(8,128)(2,1)}), bf16[32,3584]{1,0:T(8,128)(2,1)}) %reduce-scatter.2.cloned.1.call-update) | async-done | bytes 229392 | tf_op jit(solution)/shard_map/reduce_scatter | solution.py:15
  50.4 2.9 %fusion.16 = (bf16[32,3584]{1,0:T(8,128)(2,1)S(1)}, f32[32,3584]{1,0:T(8,128)}, f32[32,3584]{1,0:T(8,128)}, bf16[32,3584]{1,0:T(8,128)(2,1)}, bf16[32,3584]{1,0:T(8,128)(2,1)}) fusion(f32[32,3584]{1,0:T(8,128)} %param.12, f32[32,3584]{1,0:T(8,128)} %param.9, bf16[32,3584]{1,0:T(8,128)(2,1)} %param.11, bf16[32,3584]{1,0:T(8,128)(2,1)} %reduce-scatter.2.cloned.1.call-done, ...), kind=kLoop, calls=%fused_computation.35 | loop fusion | flops 2523136 | bytes 3211264 | tf_op jit(solution)/shard_map/convert_element_type | solution.py:71
  53.4 0.1 reshape.152
  53.5 14.2 %all_to_all.20 = bf16[4,32,896]{2,1,0:T(8,128)(2,1)} all-to-all(bf16[4,32,896]{2,1,0:T(8,128)(2,1)S(1)} %copy.28), channel_id=1, replica_groups=mesh['fsdp'=32,'dp'=4,'tensor'=4] {'dp'}, dimensions={0} | all-to-all | bytes 458752 | tf_op jit(solution)/shard_map/all_to_all | solution.py:76
  67.6 0.0 all-gather.2.cloned.1.call-update
  67.6 0.0 copy-done.2
  67.7 0.6 broadcast_in_dim.27
  68.3 8.6 %all-to-all-start = ((s32[32,1,256]{2,1,0:T(1,128)}), s32[32,1,256]{2,1,0:T(1,128)S(1)}, u32[]{:S(2)}, u32[]{:S(2)}) async-start(s32[32,1,256]{2,1,0:T(1,128)} %broadcast_in_dim.27), calls=%async_computation.1 | async-start | bytes 65536 | tf_op jit(solution)/shard_map/all_to_all | solution.py:55
  76.9 0.0 copy-done.1
  76.9 10.7 %copy.25 = bf16[8,64128]{0,1:T(8,128)(2,1)} copy(bf16[8,64128]{1,0:T(8,128)(2,1)S(1)} %copy-done.1) | data formatting | bytes 2052096 | tf_op args[5]
  87.6 0.0 all-to-all-done
  87.6 0.0 copy-start.3
  87.6 29.9 %gather_fusion = bf16[8192,8]{1,0:T(8,128)(2,1)S(1)} fusion(bf16[8,64128]{0,1:T(8,128)(2,1)} %copy.25, s32[8192]{0:T(1024)S(1)} %broadcast_clamp_fusion), kind=kCustom, calls=%fused_computation | custom fusion | bytes 294912 | tf_op jit(solution)/shard_map/gather | solution.py:58
  117.6 0.8 copy.26
  118.3 17.7 %all_to_all.21 = bf16[32,8,256]{2,1,0:T(8,128)(2,1)S(1)} all-to-all(bf16[32,8,256]{2,1,0:T(8,128)(2,1)S(1)} %bitcast.42), channel_id=1, replica_groups=mesh['fsdp'=32,'dp'=4,'tensor'=4] {'fsdp'}, dimensions={0} | all-to-all | bytes 262144 | tf_op jit(solution)/shard_map/all_to_all | solution.py:59
  136.0 16.4 %all_gather.6 = bf16[1024,256]{1,0:T(8,128)(2,1)S(1)} all-gather(bf16[256,256]{1,0:T(8,128)(2,1)S(1)} %bitcast.43), channel_id=1, replica_groups=mesh['fsdp'=32,'dp'=4,'tensor'=4] {'dp'}, dimensions={0}, use_global_device_ids=true | all-gather | bytes 655360 | tf_op jit(solution)/shard_map/all_gather | solution.py:66
  152.4 3.2 %collective-permute-start = (bf16[1024,256]{1,0:T(8,128)(2,1)S(1)}, bf16[1024,256]{1,0:T(8,128)(2,1)S(1)}, u32[]{:S(2)}, u32[]{:S(2)}) collective-permute-start(bf16[1024,256]{1,0:T(8,128)(2,1)S(1)} %all_gather.6), channel_id=1, source_target_pairs={{0,1},{1,2},{2,3},{3,0},{4,5},{5,6},{6,7},{7,4},{8,9},{9,10},{10,1... | collective-permute-start | bytes 1572872 | tf_op jit(solution)/shard_map/ppermute | solution.py:44
  155.6 3.8 %collective-permute-start.1 = (bf16[1024,256]{1,0:T(8,128)(2,1)S(1)}, bf16[1024,256]{1,0:T(8,128)(2,1)S(1)}, u32[]{:S(2)}, u32[]{:S(2)}) collective-permute-start(bf16[1024,256]{1,0:T(8,128)(2,1)S(1)} %all_gather.6), channel_id=1, source_target_pairs={{0,3},{1,0},{2,1},{3,2},{4,7},{5,4},{6,5},{7,6},{8,11},{9,8},{10,9... | collective-permute-start | bytes 1572872 | tf_op jit(solution)/shard_map/ppermute | solution.py:45
  159.5 0.0 copy-done.3
  159.5 0.1 convert_reduce_fusion
  159.6 0.1 broadcast_in_dim.26
  159.8 6.1 %collective-permute-done = bf16[1024,256]{1,0:T(8,128)(2,1)S(1)} collective-permute-done((bf16[1024,256]{1,0:T(8,128)(2,1)S(1)}, bf16[1024,256]{1,0:T(8,128)(2,1)S(1)}, u32[]{:S(2)}, u32[]{:S(2)}) %collective-permute-start) | collective-permute-done | bytes 524320 | tf_op jit(solution)/shard_map/ppermute | solution.py:44
  166.0 2.3 %collective-permute-start.2 = (bf16[512,256]{1,0:T(8,128)(2,1)S(1)}, bf16[512,256]{1,0:T(8,128)(2,1)S(1)}, u32[]{:S(2)}, u32[]{:S(2)}) collective-permute-start(bf16[512,256]{1,0:T(8,128)(2,1)S(1)} %slice.10), channel_id=1, source_target_pairs={{0,1},{1,2},{2,3},{3,0},{4,5},{5,6},{6,7},{7,4},{8,9},{9,10},{10,1... | collective-permute-start | bytes 786440 | tf_op jit(solution)/shard_map/ppermute | solution.py:48
  168.2 0.0 collective-permute-done.1
  168.3 4.8 %collective-permute-start.3 = (bf16[512,256]{1,0:T(8,128)(2,1)S(1)}, bf16[512,256]{1,0:T(8,128)(2,1)S(1)}, u32[]{:S(2)}, u32[]{:S(2)}) collective-permute-start(bf16[512,256]{1,0:T(8,128)(2,1)S(1)} %slice.11), channel_id=1, source_target_pairs={{0,3},{1,0},{2,1},{3,2},{4,7},{5,4},{6,5},{7,6},{8,11},{9,8},{10,9... | collective-permute-start | bytes 786440 | tf_op jit(solution)/shard_map/ppermute | solution.py:49
  173.2 2.3 %collective-permute-done.2 = bf16[512,256]{1,0:T(8,128)(2,1)S(1)} collective-permute-done((bf16[512,256]{1,0:T(8,128)(2,1)S(1)}, bf16[512,256]{1,0:T(8,128)(2,1)S(1)}, u32[]{:S(2)}, u32[]{:S(2)}) %collective-permute-start.2) | collective-permute-done | bytes 262176 | tf_op jit(solution)/shard_map/ppermute | solution.py:48
  175.4 1.5 collective-permute-done.3
  177.0 0.4 convert_element_type.69
  177.3 0.6 copy.27
  178.0 0.6 multiply_reduce_fusion
  178.6 0.6 fusion
  179.2 0.0 all-gather.2.cloned.1.call-done
  179.2 5.5 %fusion.17 = f32[256,896]{1,0:T(8,128)S(1)} fusion(bf16[4096,256]{1,0:T(8,128)(2,1)S(1)} %fusion, bf16[4096,896]{1,0:T(8,128)(2,1)} %all-gather.2.cloned.1.call-done), kind=kOutput, calls=%fused_computation.36 | convolution fusion | flops 1879048192 | bytes 10354688 | tf_op jit(solution)/shard_map/fk,fo->ko/dot_general | solution.py:82
  184.7 0.6 fusion.1
  185.3 0.0 copy-done
  185.3 0.2 convolution_bitcast_fusion
  185.5 12.5 %psum.14 = f32[1,8,256]{2,1,0:T(8,128)S(1)} all-reduce(f32[1,8,256]{2,1,0:T(8,128)S(1)} %convolution_bitcast_fusion), channel_id=1, replica_groups=mesh['fsdp'=32,'dp'=4,'tensor'=4] {'dp'}, use_global_device_ids=true, to_apply=%region_3.4 | all-reduce | flops 2048 | bytes 16384 | tf_op jit(solution)/shard_map/psum | solution.py:92
  198.0 12.1 %psum.15 = f32[1,8,256]{2,1,0:T(8,128)} all-reduce(f32[1,8,256]{2,1,0:T(8,128)S(1)} %psum.14), channel_id=1, replica_groups=mesh['fsdp'=32,'dp'=4,'tensor'=4] {'tensor'}, use_global_device_ids=true, to_apply=%region_4.5 | all-reduce | flops 2048 | bytes 16384 | tf_op jit(solution)/shard_map/psum | solution.py:92
  (10 shorter events, 0.3 us)
Async XLA Ops:
  7.2 178.2 %copy-start = (bf16[1,896,256]{2,1,0:T(8,128)(2,1)S(1)}, bf16[1,896,256]{2,1,0:T(8,128)(2,1)}, u32[]{:S(2)}) copy-start(bf16[1,896,256]{2,1,0:T(8,128)(2,1)} %param.17) | copy-start | bytes 1376260
  7.2 43.3 %reduce-scatter.2.cloned.1.call-start = ((), (), s32[]{:S(2)}) async-start(), calls=%async_computation.4 | async-start | bytes 1146880 | tf_op jit(solution)/shard_map/reduce_scatter | solution.py:15
  7.9 59.7 %copy-start.2 = (s32[1,256]{1,0:T(1,128)S(1)}, s32[1,256]{1,0:T(1,128)}, u32[]{:S(2)}) copy-start(s32[1,256]{1,0:T(1,128)} %param.15) | copy-start | bytes 3076
  7.9 69.0 %copy-start.1 = (bf16[8,64128]{1,0:T(8,128)(2,1)S(1)}, bf16[8,64128]{1,0:T(8,128)(2,1)}, u32[]{:S(2)}) copy-start(bf16[8,64128]{1,0:T(8,128)(2,1)} %param.14) | copy-start | bytes 3078148
  7.9 171.3 %all-gather.2.cloned.1.call-start = ((), (), s32[]{:S(2)}) async-start(), calls=%async_computation.5 | async-start | bytes 7569408 | tf_op jit(solution)/shard_map/all_gather | solution.py:77
  68.3 19.3 %all-to-all-start = ((s32[32,1,256]{2,1,0:T(1,128)}), s32[32,1,256]{2,1,0:T(1,128)S(1)}, u32[]{:S(2)}, u32[]{:S(2)}) async-start(s32[32,1,256]{2,1,0:T(1,128)} %broadcast_in_dim.27), calls=%async_computation.1 | async-start | bytes 65536 | tf_op jit(solution)/shard_map/all_to_all | solution.py:55
  87.6 71.9 %copy-start.3 = (s32[1,256]{1,0:T(1,128)S(1)}, s32[1,256]{1,0:T(1,128)}, u32[]{:S(2)}) copy-start(s32[1,256]{1,0:T(1,128)} %param.16) | copy-start | bytes 3076
  152.4 13.5 %collective-permute-start = (bf16[1024,256]{1,0:T(8,128)(2,1)S(1)}, bf16[1024,256]{1,0:T(8,128)(2,1)S(1)}, u32[]{:S(2)}, u32[]{:S(2)}) collective-permute-start(bf16[1024,256]{1,0:T(8,128)(2,1)S(1)} %all_gather.6), channel_id=1, source_target_pairs={{0,1},{1,2},{2,3},{3,0},{4,5},{5,6},{6,7},{7,4},{8,9},{9,10},{10,1... | collective-permute-start | bytes 1572872 | tf_op jit(solution)/shard_map/ppermute | solution.py:44
  155.6 12.6 %collective-permute-start.1 = (bf16[1024,256]{1,0:T(8,128)(2,1)S(1)}, bf16[1024,256]{1,0:T(8,128)(2,1)S(1)}, u32[]{:S(2)}, u32[]{:S(2)}) collective-permute-start(bf16[1024,256]{1,0:T(8,128)(2,1)S(1)} %all_gather.6), channel_id=1, source_target_pairs={{0,3},{1,0},{2,1},{3,2},{4,7},{5,4},{6,5},{7,6},{8,11},{9,8},{10,9... | collective-permute-start | bytes 1572872 | tf_op jit(solution)/shard_map/ppermute | solution.py:45
  166.0 9.5 %collective-permute-start.2 = (bf16[512,256]{1,0:T(8,128)(2,1)S(1)}, bf16[512,256]{1,0:T(8,128)(2,1)S(1)}, u32[]{:S(2)}, u32[]{:S(2)}) collective-permute-start(bf16[512,256]{1,0:T(8,128)(2,1)S(1)} %slice.10), channel_id=1, source_target_pairs={{0,1},{1,2},{2,3},{3,0},{4,5},{5,6},{6,7},{7,4},{8,9},{9,10},{10,1... | collective-permute-start | bytes 786440 | tf_op jit(solution)/shard_map/ppermute | solution.py:48
  168.3 8.7 %collective-permute-start.3 = (bf16[512,256]{1,0:T(8,128)(2,1)S(1)}, bf16[512,256]{1,0:T(8,128)(2,1)S(1)}, u32[]{:S(2)}, u32[]{:S(2)}) collective-permute-start(bf16[512,256]{1,0:T(8,128)(2,1)S(1)} %slice.11), channel_id=1, source_target_pairs={{0,3},{1,0},{2,1},{3,2},{4,7},{5,4},{6,5},{7,6},{8,11},{9,8},{10,9... | collective-permute-start | bytes 786440 | tf_op jit(solution)/shard_map/ppermute | solution.py:49
Sparse Core Ops, SparseCore 0:
  10.8 39.5 reduce-scatter.1
  67.8 72.7 all-gather.1
where the time goes:
time: 217 us
  blocking collectives  72.8 us (34%)
  waiting for transfers between devices  53.1 us (24%)
  local copies, waits for them, and re-layouts  43 us (20%)
  starting transfers between devices  22.8 us (11%)
  between operations  14.3 us (7%)
  matrix products  6.27 us (3%)
  other arithmetic  4.68 us (2%)
    reduce_scatter x1, waiting for transfers between devices, optimizer_step(): lax.psum_scatter(grad_parts[0], 'dp', scatter_dimension=0, tiled=True)  42.5 us
    gather x1, local copies, waits for them, and re-layouts, embed_inputs(): embed_table.at[:, every_id.reshape(-1)].get(mode='promise_in_bounds')  29.9 us
    psum x2, blocking collectives, label_tokens(): return lax.psum(lax.psum(partial_terms, 'dp'), 'tensor')  24.6 us
    all_to_all x1, blocking collectives, embed_inputs(): lax.all_to_all(picked.reshape(8, 32, 256).transpose(1, 0, 2), 'fsdp', spl...  17.7 us
    all_gather x1, blocking collectives, embed_inputs(): part = lax.all_gather(received.reshape(256, 256), 'dp', axis=0, tiled=True)  16.4 us
    all_to_all x1, blocking collectives, label_tokens(): block = lax.all_to_all(split.reshape(-1, width), 'dp', 0, 0, tiled=True)  14.2 us
    unnamed x9, local copies, waits for them, and re-layouts  10.7 us
    all_to_all x1, starting transfers between devices, embed_inputs(): lax.all_to_all(jnp.broadcast_to(token_ids, (32, token_ids.shape[1])), 'fs...  8.59 us
  transfers between devices with their start and end apart: 7, of which 4 were waited for; matrix products, arithmetic and copies ran while one was open for 21% of the time, Pallas kernels for 0%

commit v1 on v0

--- a/solution.py
+++ b/solution.py
@@ -89,7 +89,7 @@
     pooled = (totals / jnp.sum(member_of, axis=2, keepdims=True)).astype(jnp.bfloat16)
     head_part = class_head[0]
     partial_terms = jnp.einsum("gpk,kc->gpc", pooled, head_part, preferred_element_type=jnp.float32)
-    return lax.psum(lax.psum(partial_terms, "dp"), "tensor")
+    return jnp.sum(lax.all_gather(lax.psum(partial_terms, "dp"), "tensor"), axis=0)
 
 
 def shards(

time: 217 us -> 219 us (level)
  the two profiles are of different devices: /device:TPU:8 before, /device:TPU:10 now
where the time goes in v1:
time: 219 us; the launch traced here: 218 us
  blocking collectives  74.4 us (34%)
  waiting for transfers between devices  54.3 us (25%)
  local copies, waits for them, and re-layouts  43 us (20%)
  starting transfers between devices  20.8 us (9%)
  between operations  14.3 us (7%)
  matrix products  6.27 us (3%)
  other arithmetic  5.28 us (2%)
    reduce_scatter x1, waiting for transfers between devices, optimizer_step(): lax.psum_scatter(grad_parts[0], 'dp', scatter_dimension=0, tiled=True)  41.4 us
    gather x1, local copies, waits for them, and re-layouts, embed_inputs(): embed_table.at[:, every_id.reshape(-1)].get(mode='promise_in_bounds')  29.9 us
    all_to_all x1, blocking collectives, embed_inputs(): lax.all_to_all(picked.reshape(8, 32, 256).transpose(1, 0, 2), 'fsdp', spl...  17.7 us
    all_gather x1, blocking collectives, embed_inputs(): part = lax.all_gather(received.reshape(256, 256), 'dp', axis=0, tiled=True)  16.2 us
    all_to_all x1, blocking collectives, label_tokens(): block = lax.all_to_all(split.reshape(-1, width), 'dp', 0, 0, tiled=True)  14.7 us
    all_gather x1, blocking collectives, label_tokens(): lax.all_gather(lax.psum(partial_terms, 'dp'), 'tensor')  13.5 us
    psum x1, blocking collectives, label_tokens(): lax.psum(partial_terms, 'dp')  12.3 us
    unnamed x9, local copies, waits for them, and re-layouts  10.7 us
  transfers between devices with their start and end apart: 7, of which 4 were waited for; matrix products, arithmetic and copies ran while one was open for 20% of the time, Pallas kernels for 0%

profile of v1, /device:TPU:10, one launch (start us, length us, event | category | flops | bytes accessed | tf_op | source)
XLA Modules:
  0.0 218.4 jit_solution(6358296071925762459)
XLA Ops:
  7.2 0.0 copy-start
  7.2 0.0 reduce-scatter.2.cloned.1.call-start
  7.2 0.7 reduce-scatter.2.cloned.1.call-update
  7.9 0.0 copy-start.2
  7.9 0.0 copy-start.1
  7.9 0.0 all-gather.2.cloned.1.call-start
  8.0 41.4 %reduce-scatter.2.cloned.1.call-done = bf16[32,3584]{1,0:T(8,128)(2,1)} async-done(((bf16[128,3584]{1,0:T(8,128)(2,1)}), bf16[32,3584]{1,0:T(8,128)(2,1)}) %reduce-scatter.2.cloned.1.call-update) | async-done | bytes 229392 | tf_op jit(solution)/shard_map/reduce_scatter | solution.py:15
  49.4 2.9 %fusion.16 = (bf16[32,3584]{1,0:T(8,128)(2,1)S(1)}, f32[32,3584]{1,0:T(8,128)}, f32[32,3584]{1,0:T(8,128)}, bf16[32,3584]{1,0:T(8,128)(2,1)}, bf16[32,3584]{1,0:T(8,128)(2,1)}) fusion(f32[32,3584]{1,0:T(8,128)} %param.12, f32[32,3584]{1,0:T(8,128)} %param.9, bf16[32,3584]{1,0:T(8,128)(2,1)} %param.11, bf16[32,3584]{1,0:T(8,128)(2,1)} %reduce-scatter.2.cloned.1.call-done, ...), kind=kLoop, calls=%fused_computation.35 | loop fusion | flops 2523136 | bytes 3211264 | tf_op jit(solution)/shard_map/convert_element_type | solution.py:71
  52.3 0.1 reshape.153
  52.4 14.7 %all_to_all.20 = bf16[4,32,896]{2,1,0:T(8,128)(2,1)} all-to-all(bf16[4,32,896]{2,1,0:T(8,128)(2,1)S(1)} %copy.28), channel_id=1, replica_groups=mesh['fsdp'=32,'dp'=4,'tensor'=4] {'dp'}, dimensions={0} | all-to-all | bytes 458752 | tf_op jit(solution)/shard_map/all_to_all | solution.py:76
  67.1 0.0 all-gather.2.cloned.1.call-update
  67.1 0.0 copy-done.2
  67.2 0.6 broadcast_in_dim.27
  67.8 9.1 %all-to-all-start = ((s32[32,1,256]{2,1,0:T(1,128)}), s32[32,1,256]{2,1,0:T(1,128)S(1)}, u32[]{:S(2)}, u32[]{:S(2)}) async-start(s32[32,1,256]{2,1,0:T(1,128)} %broadcast_in_dim.27), calls=%async_computation.1 | async-start | bytes 65536 | tf_op jit(solution)/shard_map/all_to_all | solution.py:55
  76.9 0.0 copy-done.1
  76.9 10.7 %copy.25 = bf16[8,64128]{0,1:T(8,128)(2,1)} copy(bf16[8,64128]{1,0:T(8,128)(2,1)S(1)} %copy-done.1) | data formatting | bytes 2052096 | tf_op args[5]
  87.6 0.0 all-to-all-done
  87.6 0.0 copy-start.3
  87.6 29.9 %gather_fusion = bf16[8192,8]{1,0:T(8,128)(2,1)S(1)} fusion(bf16[8,64128]{0,1:T(8,128)(2,1)} %copy.25, s32[8192]{0:T(1024)S(1)} %broadcast_clamp_fusion), kind=kCustom, calls=%fused_computation | custom fusion | bytes 294912 | tf_op jit(solution)/shard_map/gather | solution.py:58
  117.6 0.8 copy.26
  118.3 17.7 %all_to_all.21 = bf16[32,8,256]{2,1,0:T(8,128)(2,1)S(1)} all-to-all(bf16[32,8,256]{2,1,0:T(8,128)(2,1)S(1)} %bitcast.43), channel_id=1, replica_groups=mesh['fsdp'=32,'dp'=4,'tensor'=4] {'fsdp'}, dimensions={0} | all-to-all | bytes 262144 | tf_op jit(solution)/shard_map/all_to_all | solution.py:59
  136.0 16.2 %all_gather.12 = bf16[1024,256]{1,0:T(8,128)(2,1)S(1)} all-gather(bf16[256,256]{1,0:T(8,128)(2,1)S(1)} %bitcast.44), channel_id=1, replica_groups=mesh['fsdp'=32,'dp'=4,'tensor'=4] {'dp'}, dimensions={0}, use_global_device_ids=true | all-gather | bytes 655360 | tf_op jit(solution)/shard_map/all_gather | solution.py:66
  152.2 3.3 %collective-permute-start = (bf16[1024,256]{1,0:T(8,128)(2,1)S(1)}, bf16[1024,256]{1,0:T(8,128)(2,1)S(1)}, u32[]{:S(2)}, u32[]{:S(2)}) collective-permute-start(bf16[1024,256]{1,0:T(8,128)(2,1)S(1)} %all_gather.12), channel_id=1, source_target_pairs={{0,1},{1,2},{2,3},{3,0},{4,5},{5,6},{6,7},{7,4},{8,9},{9,10},{10,1... | collective-permute-start | bytes 1572872 | tf_op jit(solution)/shard_map/ppermute | solution.py:44
  155.5 2.5 %collective-permute-start.1 = (bf16[1024,256]{1,0:T(8,128)(2,1)S(1)}, bf16[1024,256]{1,0:T(8,128)(2,1)S(1)}, u32[]{:S(2)}, u32[]{:S(2)}) collective-permute-start(bf16[1024,256]{1,0:T(8,128)(2,1)S(1)} %all_gather.12), channel_id=1, source_target_pairs={{0,3},{1,0},{2,1},{3,2},{4,7},{5,4},{6,5},{7,6},{8,11},{9,8},{10,9... | collective-permute-start | bytes 1572872 | tf_op jit(solution)/shard_map/ppermute | solution.py:45
  158.1 0.0 copy-done.3
  158.1 0.1 convert_reduce_fusion
  158.2 0.1 broadcast_in_dim.26
  158.4 6.4 %collective-permute-done = bf16[1024,256]{1,0:T(8,128)(2,1)S(1)} collective-permute-done((bf16[1024,256]{1,0:T(8,128)(2,1)S(1)}, bf16[1024,256]{1,0:T(8,128)(2,1)S(1)}, u32[]{:S(2)}, u32[]{:S(2)}) %collective-permute-start) | collective-permute-done | bytes 524320 | tf_op jit(solution)/shard_map/ppermute | solution.py:44
  164.8 3.4 %collective-permute-start.2 = (bf16[512,256]{1,0:T(8,128)(2,1)S(1)}, bf16[512,256]{1,0:T(8,128)(2,1)S(1)}, u32[]{:S(2)}, u32[]{:S(2)}) collective-permute-start(bf16[512,256]{1,0:T(8,128)(2,1)S(1)} %slice.10), channel_id=1, source_target_pairs={{0,1},{1,2},{2,3},{3,0},{4,5},{5,6},{6,7},{7,4},{8,9},{9,10},{10,1... | collective-permute-start | bytes 786440 | tf_op jit(solution)/shard_map/ppermute | solution.py:48
  168.2 0.0 collective-permute-done.1
  168.3 2.4 %collective-permute-start.3 = (bf16[512,256]{1,0:T(8,128)(2,1)S(1)}, bf16[512,256]{1,0:T(8,128)(2,1)S(1)}, u32[]{:S(2)}, u32[]{:S(2)}) collective-permute-start(bf16[512,256]{1,0:T(8,128)(2,1)S(1)} %slice.11), channel_id=1, source_target_pairs={{0,3},{1,0},{2,1},{3,2},{4,7},{5,4},{6,5},{7,6},{8,11},{9,8},{10,9... | collective-permute-start | bytes 786440 | tf_op jit(solution)/shard_map/ppermute | solution.py:49
  170.8 2.3 %collective-permute-done.2 = bf16[512,256]{1,0:T(8,128)(2,1)S(1)} collective-permute-done((bf16[512,256]{1,0:T(8,128)(2,1)S(1)}, bf16[512,256]{1,0:T(8,128)(2,1)S(1)}, u32[]{:S(2)}, u32[]{:S(2)}) %collective-permute-start.2) | collective-permute-done | bytes 262176 | tf_op jit(solution)/shard_map/ppermute | solution.py:48
  173.1 3.5 %collective-permute-done.3 = bf16[512,256]{1,0:T(8,128)(2,1)S(1)} collective-permute-done((bf16[512,256]{1,0:T(8,128)(2,1)S(1)}, bf16[512,256]{1,0:T(8,128)(2,1)S(1)}, u32[]{:S(2)}, u32[]{:S(2)}) %collective-permute-start.3) | collective-permute-done | bytes 262176 | tf_op jit(solution)/shard_map/ppermute | solution.py:49
  176.6 0.4 convert_element_type.69
  177.0 0.6 copy.27
  177.6 0.6 multiply_reduce_fusion
  178.2 0.6 fusion
  178.8 0.0 all-gather.2.cloned.1.call-done
  178.8 5.5 %fusion.17 = f32[256,896]{1,0:T(8,128)S(1)} fusion(bf16[4096,256]{1,0:T(8,128)(2,1)S(1)} %fusion, bf16[4096,896]{1,0:T(8,128)(2,1)} %all-gather.2.cloned.1.call-done), kind=kOutput, calls=%fused_computation.36 | convolution fusion | flops 1879048192 | bytes 10354688 | tf_op jit(solution)/shard_map/fk,fo->ko/dot_general | solution.py:82
  184.3 0.6 fusion.1
  184.9 0.0 copy-done
  184.9 0.2 convolution_bitcast_fusion
  185.1 12.3 %psum.7 = f32[1,1,8,256]{3,2,1,0:T(8,128)S(1)} all-reduce(f32[1,1,8,256]{3,2,1,0:T(8,128)S(1)} %convolution_bitcast_fusion), channel_id=1, replica_groups=mesh['fsdp'=32,'dp'=4,'tensor'=4] {'dp'}, use_global_device_ids=true, to_apply=%region_3.4 | all-reduce | flops 2048 | bytes 16384 | tf_op jit(solution)/shard_map/psum | solution.py:92
  197.5 13.5 %all_gather.15 = f32[4,1,8,256]{3,2,1,0:T(8,128)S(1)} all-gather(f32[1,1,8,256]{3,2,1,0:T(8,128)S(1)} %psum.7), channel_id=1, replica_groups=mesh['fsdp'=32,'dp'=4,'tensor'=4] {'tensor'}, dimensions={0}, use_global_device_ids=true | all-gather | bytes 40960 | tf_op jit(solution)/shard_map/all_gather | solution.py:92
  210.9 0.6 reduce_sum.31
  (10 shorter events, 0.3 us)
Async XLA Ops:
  7.2 177.8 %copy-start = (bf16[1,896,256]{2,1,0:T(8,128)(2,1)S(1)}, bf16[1,896,256]{2,1,0:T(8,128)(2,1)}, u32[]{:S(2)}) copy-start(bf16[1,896,256]{2,1,0:T(8,128)(2,1)} %param.17) | copy-start | bytes 1376260
  7.2 42.2 %reduce-scatter.2.cloned.1.call-start = ((), (), s32[]{:S(2)}) async-start(), calls=%async_computation.4 | async-start | bytes 1146880 | tf_op jit(solution)/shard_map/reduce_scatter | solution.py:15
  7.9 59.2 %copy-start.2 = (s32[1,256]{1,0:T(1,128)S(1)}, s32[1,256]{1,0:T(1,128)}, u32[]{:S(2)}) copy-start(s32[1,256]{1,0:T(1,128)} %param.15) | copy-start | bytes 3076
  7.9 69.0 %copy-start.1 = (bf16[8,64128]{1,0:T(8,128)(2,1)S(1)}, bf16[8,64128]{1,0:T(8,128)(2,1)}, u32[]{:S(2)}) copy-start(bf16[8,64128]{1,0:T(8,128)(2,1)} %param.14) | copy-start | bytes 3078148
  7.9 170.9 %all-gather.2.cloned.1.call-start = ((), (), s32[]{:S(2)}) async-start(), calls=%async_computation.5 | async-start | bytes 7569408 | tf_op jit(solution)/shard_map/all_gather | solution.py:77
  67.8 19.8 %all-to-all-start = ((s32[32,1,256]{2,1,0:T(1,128)}), s32[32,1,256]{2,1,0:T(1,128)S(1)}, u32[]{:S(2)}, u32[]{:S(2)}) async-start(s32[32,1,256]{2,1,0:T(1,128)} %broadcast_in_dim.27), calls=%async_computation.1 | async-start | bytes 65536 | tf_op jit(solution)/shard_map/all_to_all | solution.py:55
  87.6 70.5 %copy-start.3 = (s32[1,256]{1,0:T(1,128)S(1)}, s32[1,256]{1,0:T(1,128)}, u32[]{:S(2)}) copy-start(s32[1,256]{1,0:T(1,128)} %param.16) | copy-start | bytes 3076
  152.2 12.6 %collective-permute-start = (bf16[1024,256]{1,0:T(8,128)(2,1)S(1)}, bf16[1024,256]{1,0:T(8,128)(2,1)S(1)}, u32[]{:S(2)}, u32[]{:S(2)}) collective-permute-start(bf16[1024,256]{1,0:T(8,128)(2,1)S(1)} %all_gather.12), channel_id=1, source_target_pairs={{0,1},{1,2},{2,3},{3,0},{4,5},{5,6},{6,7},{7,4},{8,9},{9,10},{10,1... | collective-permute-start | bytes 1572872 | tf_op jit(solution)/shard_map/ppermute | solution.py:44
  155.5 12.7 %collective-permute-start.1 = (bf16[1024,256]{1,0:T(8,128)(2,1)S(1)}, bf16[1024,256]{1,0:T(8,128)(2,1)S(1)}, u32[]{:S(2)}, u32[]{:S(2)}) collective-permute-start(bf16[1024,256]{1,0:T(8,128)(2,1)S(1)} %all_gather.12), channel_id=1, source_target_pairs={{0,3},{1,0},{2,1},{3,2},{4,7},{5,4},{6,5},{7,6},{8,11},{9,8},{10,9... | collective-permute-start | bytes 1572872 | tf_op jit(solution)/shard_map/ppermute | solution.py:45
  164.8 8.3 %collective-permute-start.2 = (bf16[512,256]{1,0:T(8,128)(2,1)S(1)}, bf16[512,256]{1,0:T(8,128)(2,1)S(1)}, u32[]{:S(2)}, u32[]{:S(2)}) collective-permute-start(bf16[512,256]{1,0:T(8,128)(2,1)S(1)} %slice.10), channel_id=1, source_target_pairs={{0,1},{1,2},{2,3},{3,0},{4,5},{5,6},{6,7},{7,4},{8,9},{9,10},{10,1... | collective-permute-start | bytes 786440 | tf_op jit(solution)/shard_map/ppermute | solution.py:48
  168.3 8.3 %collective-permute-start.3 = (bf16[512,256]{1,0:T(8,128)(2,1)S(1)}, bf16[512,256]{1,0:T(8,128)(2,1)S(1)}, u32[]{:S(2)}, u32[]{:S(2)}) collective-permute-start(bf16[512,256]{1,0:T(8,128)(2,1)S(1)} %slice.11), channel_id=1, source_target_pairs={{0,3},{1,0},{2,1},{3,2},{4,7},{5,4},{6,5},{7,6},{8,11},{9,8},{10,9... | collective-permute-start | bytes 786440 | tf_op jit(solution)/shard_map/ppermute | solution.py:49
Sparse Core Ops, SparseCore 0:
  10.8 38.5 reduce-scatter.1
  67.3 73.2 all-gather.1
